TPU v7x, 32 devices: a whole 2x2x4 slice. The times are simulated.
32 devices in a mesh: sector: 4 (over z), axial: 8 (over y, x, core).
Axes of the slice: x: 2, y: 2, z: 4, core: 2. Of those that a mesh axis runs over, the one named last changes fastest.
Arguments:
- kbb: float32 [4096, 64, 64], P(('sector', 'axial')), as said below
- interior: bfloat16 [4096, 256, 64], P(('sector', 'axial')), may hold values from -0.075683594 to 0.075683594
- node_lists: int32 [4096, 64], P(('sector', 'axial')), may hold values from -1 to 63
- owners: int32 [4096, 1], P(('sector', 'axial')), may hold values from 0 to 31; in each aligned block of 128 rows (0 to 127, 128 to 255, ...) at most 8 rows name the same one
- patch_ids: int32 [4096], P(('sector', 'axial')), may hold values from 0 to 63
- counts: int32 [32], P(('sector', 'axial')), may hold values from 96 to 128
- capacity: float32 [131072], P(('sector', 'axial')), may hold values from 0.2 to 2
- links: int32 [2, 512, 2], P(None, ('sector', 'axial')), may hold values from 0 to 63
- conduct: float32 [2, 512, 64], P(None, ('sector', 'axial')), may hold values from 0.5 to 4
- loads: float32 [131072, 128], P(('sector', 'axial')), may hold values from -24 to 24
Outputs:
- current_estimate: float32 [131072, 128], P(('sector', 'axial'))
- remaining_imbalance: float32 [131072, 128], P(('sector', 'axial'))
Inputs may be any that keep to these rules, and one draw needn't show every extreme that they name: `owners`: no owner is named by more than 8 of one device's slots, live or not, and in every draw some owner is named by exactly 8 of some device's slots. The live slots of a device are its first counts slots; the others are padding. `kbb`: the boundary block is symmetric with non-positive entries off the diagonal whose row sums stay under its diagonal.
All inputs are finite; a program needn't handle non-finite values.
Results may differ from a plain program's by a relative error of at most 0.0003.
Values sent between devices are 32-bit elements; how exact they have to be, the bound alone decides.
No kernel may reach another device: no remote copies, remote signals or barrier semaphores. Data moves between devices by JAX's collectives and lax.ppermute only.
A program may use at most 128 MiB of HBM per device.

v0:
```python
import jax
import jax.numpy as jnp
from jax import lax
from jax.sharding import PartitionSpec as P

ITERS = 3
highest = lax.Precision.HIGHEST


def from_behind(array, axis, by):
    length = lax.axis_size(axis)
    return lax.ppermute(array, axis, [(i, (i + by) % length) for i in range(length)])


def shifted(block, axis, distance):
    devices = range(lax.axis_size(axis))
    route = [(i - distance, i) for i in devices if i - distance in devices]
    return lax.ppermute(block, axis, route)


def onehot_rows(index, count):
    return (index[:, None] == jnp.arange(count, dtype=jnp.int32)[None, :]).astype(jnp.float32)


def spread_field(index, values, count):
    return jnp.einsum("lp,lir->pir", onehot_rows(index, count), values, precision=highest)


def spread_flat(index, values, count):
    return jnp.einsum("lp,li->pi", onehot_rows(index, count), values, precision=highest)


def shards(kbb, interior, node_lists, owners, patch_ids, counts, capacity, links, conduct, loads):
    elem_slots, bound_nodes = node_lists.shape
    devices = lax.axis_size("sector") * lax.axis_size("axial")
    slots_each = 2 * elem_slots // devices
    total_slots = devices * slots_each
    points_in_partition, scenario_vectors = loads.shape
    patch_dev = points_in_partition // bound_nodes
    schur = kbb - jnp.einsum("eib,eic->ebc", interior, interior, preferred_element_type=jnp.float32)
    live = (jnp.arange(elem_slots, dtype=jnp.int32) < counts[0]).astype(jnp.int32)
    owner_hot = onehot_rows(owners[:, 0], devices)
    ranks = jnp.sum(jnp.cumsum(owner_hot, axis=0) * owner_hot, axis=1).astype(jnp.int32) - 1
    target = owners[:, 0] * slots_each + ranks
    send_blocks = (
        jnp.zeros((total_slots, bound_nodes, bound_nodes), jnp.float32).at[target].set(schur)
    )
    send_nodes = jnp.full((total_slots, bound_nodes), -1, jnp.int32).at[target].set(node_lists)
    send_patch = jnp.zeros((total_slots,), jnp.int32).at[target].set(patch_ids)
    send_live = jnp.zeros((total_slots,), jnp.int32).at[target].set(live)
    blocks_in, nodes_in, patch_in, live_in = (
        lax.all_to_all(send_blocks, ("sector", "axial"), split_axis=0, concat_axis=0, tiled=True),
        lax.all_to_all(send_nodes, ("sector", "axial"), split_axis=0, concat_axis=0, tiled=True),
        lax.all_to_all(send_patch, ("sector", "axial"), split_axis=0, concat_axis=0, tiled=True),
        lax.all_to_all(send_live, ("sector", "axial"), split_axis=0, concat_axis=0, tiled=True),
    )
    picker = (
        nodes_in[:, :, None] == jnp.arange(bound_nodes, dtype=jnp.int32)[None, None, :]
    ).astype(jnp.float32)
    half = jnp.einsum("rsj,rst->rjt", picker, blocks_in, precision=highest)
    placed = jnp.einsum("rjt,rtk->rjk", half, picker, precision=highest)
    weights = onehot_rows(patch_in, patch_dev) * live_in[:, None].astype(jnp.float32)
    assembled = jnp.einsum("rp,rjk->pjk", weights, placed, precision=highest)
    sector_own = links[0, :, 0]
    sector_far = links[0, :, 1]
    sector_gain = conduct[0]
    axial_own = links[1, :, 0]
    axial_far = links[1, :, 1]
    axial_gain = conduct[1]
    sector_in_far, sector_in_gain = from_behind((sector_far, sector_gain), "sector", 1)
    axial_in_far, axial_in_gain = shifted((axial_far, axial_gain), "axial", 1)
    heat = capacity.reshape(patch_dev, bound_nodes)
    diagonal = heat + jnp.diagonal(assembled, axis1=1, axis2=2)
    diagonal = (
        diagonal
        + spread_flat(sector_own, sector_gain, patch_dev)
        + spread_flat(sector_in_far, sector_in_gain, patch_dev)
    )
    diagonal = (
        diagonal
        + spread_flat(axial_own, axial_gain, patch_dev)
        + spread_flat(axial_in_far, axial_in_gain, patch_dev)
    )

    def precond_sum(remaining_imbalance, precond):
        return lax.psum(jnp.sum(remaining_imbalance * precond, axis=(0, 1)), ("sector", "axial"))

    remaining_imbalance = loads.reshape(patch_dev, bound_nodes, scenario_vectors)
    current_estimate = jnp.zeros_like(remaining_imbalance)
    scale = diagonal[:, :, None]
    precond = remaining_imbalance / scale
    update_vector = precond
    norm_now = precond_sum(remaining_imbalance, precond)
    for sweep in range(ITERS):
        result = heat[:, :, None] * update_vector + jnp.einsum(
            "pij,pjr->pir", assembled, update_vector, precision=highest
        )
        beyond = from_behind(update_vector[sector_in_far], "sector", -1)
        flux = sector_gain[:, :, None] * (update_vector[sector_own] - beyond)
        passed = from_behind(flux, "sector", 1)
        result = (
            result
            + spread_field(sector_own, flux, patch_dev)
            - spread_field(sector_in_far, passed, patch_dev)
        )
        beyond = shifted(update_vector[axial_in_far], "axial", -1)
        flux = axial_gain[:, :, None] * (update_vector[axial_own] - beyond)
        passed = shifted(flux, "axial", 1)
        result = (
            result
            + spread_field(axial_own, flux, patch_dev)
            - spread_field(axial_in_far, passed, patch_dev)
        )
        update_factor = norm_now / lax.psum(
            jnp.sum(update_vector * result, axis=(0, 1)), ("sector", "axial")
        )
        current_estimate = current_estimate + update_factor * update_vector
        remaining_imbalance = remaining_imbalance - update_factor * result
        if sweep + 1 < ITERS:
            precond = remaining_imbalance / scale
            norm_next = precond_sum(remaining_imbalance, precond)
            update_vector = precond + norm_next / norm_now * update_vector
            norm_now = norm_next
    return (
        current_estimate.reshape(points_in_partition, scenario_vectors),
        remaining_imbalance.reshape(points_in_partition, scenario_vectors),
    )


def solution(mesh):
    placed = (
        P(("sector", "axial"), None, None),
        P(("sector", "axial"), None, None),
        P(("sector", "axial"), None),
        P(("sector", "axial"), None),
        P(("sector", "axial")),
        P(("sector", "axial")),
        P(("sector", "axial")),
        P(None, ("sector", "axial"), None),
        P(None, ("sector", "axial"), None),
        P(("sector", "axial"), None),
    )
    return jax.shard_map(
        shards,
        mesh=mesh,
        in_specs=placed,
        out_specs=(P(("sector", "axial"), None), P(("sector", "axial"), None)),
        check_vma=False,
    )
```

profile of v0, /device:TPU:10, one launch (start us, length us, event | category | flops | bytes accessed | tf_op | source)
XLA Modules:
  0.0 622.8 jit_solution(7202846408577687185)
XLA Ops:
  5.4 6.0 all-to-all-start.1
  16.4 4.6 all-to-all-start
  21.0 5.6 copy.75
  28.3 5.9 all-to-all-start.2
  34.2 7.9 %convolution_subtract_fusion = f32[128,64,64]{2,1,0:T(8,128)} fusion(f32[128,64,64]{2,1,0:T(8,128)} %copy.75, bf16[128,256,64]{1,2,0:T(8,128)(2,1)} %param.11), kind=kOutput, calls=%fused_computation.25 | convolution fusion | flops 268959744 | bytes 8388608 | tf_op jit(solution)/shard_map/eib,eic->ebc/dot_general | solution.py:40
  42.1 4.3 broadcast_in_dim.11
  46.4 19.3 %scatter_fusion = f32[256,64,64]{2,1,0:T(8,128)} fusion(f32[256,64,64]{2,1,0:T(8,128)} %broadcast_in_dim.11, s32[128]{0:T(128)S(1)} %fusion.85, f32[128,64,64]{2,1,0:T(8,128)} %convolution_subtract_fusion), kind=kCustom, calls=%fused_computation.16 | custom fusion | bytes 6291968 | tf_op jit(solution)/shard_map/scatter | solution.py:46
  65.7 9.8 %reshape.288 = f32[32,1,32768]{2,1,0:T(1,128)} reshape(f32[256,64,64]{2,1,0:T(8,128)} %scatter_fusion) | data formatting | bytes 8388608
  75.6 5.9 all-to-all-start.3
  90.4 13.4 %collective-permute-done.2 = s32[16]{0:T(128)S(1)} collective-permute-done((s32[16]{0:T(128)S(1)}, s32[16]{0:T(128)S(1)}, u32[]{:S(2)}, u32[]{:S(2)}) %collective-permute-start.2) | collective-permute-done | bytes 96 | tf_op jit(solution)/shard_map/ppermute | solution.py:18
  106.6 65.6 %all-to-all-done.3 = f32[32,1,32768]{2,1,0:T(1,128)} async-done(((f32[32,1,32768]{2,1,0:T(1,128)}), f32[32,1,32768]{2,1,0:T(1,128)}, u32[]{:S(2)}, u32[]{:S(2)}) %all-to-all-start.3) | async-done | bytes 4194336 | tf_op jit(solution)/shard_map/all_to_all | solution.py:52
  172.7 13.7 %reduce.9 = f32[32,32768]{1,0:T(8,128)} reduce(f32[32,1,32768]{2,1,0:T(1,128)} %all-to-all-done.3, f32[]{:T(128)} %broadcast.166), dimensions={1}, to_apply=%all_to_all.27.reduce_sub_computation | reduce | bytes 8388612 | tf_op jit(solution)/shard_map/all_to_all | solution.py:52
  186.5 7.4 %reshape.289 = f32[256,64,64]{2,1,0:T(8,128)} reshape(f32[32,32768]{1,0:T(8,128)} %reduce.9) | data formatting | bytes 8388608
  193.8 11.8 %fusion.3 = f32[256,64,64]{2,1,0:T(8,128)S(1)} fusion(f32[256,64,64]{2,1,0:T(8,128)} %reshape.289, s32[256,64]{1,0:T(8,128)S(1)} %bitcast.83), kind=kOutput, calls=%fused_computation.21 | convolution fusion | flops 806354944 | bytes 8454144 | tf_op jit(solution)/shard_map/rsj,rst->rjt/dot_general | solution.py:60
  205.7 8.2 %fusion.2 = f32[256,64,64]{2,1,0:T(8,128)S(1)} fusion(f32[256,64,64]{2,1,0:T(8,128)S(1)} %fusion.3, s32[256,64]{1,0:T(8,128)S(1)} %bitcast.84), kind=kOutput, calls=%fused_computation.20 | convolution fusion | flops 806354944 | bytes 8454144 | tf_op jit(solution)/shard_map/rjt,rtk->rjk/dot_general | solution.py:61
  213.8 11.0 %fusion = f32[64,64,64]{2,0,1:T(8,128)} fusion(f32[256,64,64]{2,1,0:T(8,128)S(1)} %fusion.2, f32[256]{0:T(256)S(1)} %convert_element_type.50, s32[256]{0:T(256)S(1)} %eq.56), kind=kOutput, calls=%fused_computation.17 | convolution fusion | flops 805339136 | bytes 5244928 | tf_op jit(solution)/shard_map/rp,rjk->pjk/dot_general | solution.py:63
  252.1 8.1 %collective-permute-done.4 = f32[16,64,128]{2,1,0:T(8,128)S(1)} collective-permute-done((f32[16,64,128]{2,1,0:T(8,128)}, f32[16,64,128]{2,1,0:T(8,128)S(1)}, u32[]{:S(2)}, u32[]{:S(2)}) %collective-permute-start.4) | collective-permute-done | bytes 524320 | tf_op jit(solution)/shard_map/ppermute | solution.py:12
  265.6 9.5 %collective-permute-done.5 = f32[16,64,128]{2,1,0:T(8,128)S(1)} collective-permute-done((f32[16,64,128]{2,1,0:T(8,128)S(1)}, f32[16,64,128]{2,1,0:T(8,128)S(1)}, u32[]{:S(2)}, u32[]{:S(2)}) %collective-permute-start.5) | collective-permute-done | bytes 524320 | tf_op jit(solution)/shard_map/ppermute | solution.py:12
  276.2 13.9 %multiply_reduce_fusion.4 = (f32[128]{0:T(128)S(1)}, f32[64,64,128]{2,1,0:T(8,128)}) fusion(f32[64,64,128]{2,1,0:T(8,128)S(1)} %copy-done.6, f32[64,64,128]{2,0,1:T(8,128)S(1)} %fusion.36, f32[64,64,128]{2,0,1:T(8,128)S(1)} %fusion.38, f32[64,64,128]{2,0,1:T(8,128)S(1)} %fusion.40, f32[64,64,128]{2,0,1:T(8,128)S(1)} %fusion.42, ...), kind=kOutput, calls=%fused_computation.48 | convolution fusion | flops 406847360 | bytes 13648384 | tf_op jit(solution)/shard_map/pij,pjr->pir/dot_general | solution.py:95
  290.1 43.9 %all-reduce = (f32[128]{0:T(128)S(1)}, f32[128]{0:T(128)S(1)}) all-reduce(f32[128]{0:T(128)S(1)} %fusion.6, f32[128]{0:T(128)S(1)} %get-tuple-element.18), channel_id=1, replica_groups=mesh['sector'=4,'axial'=8] {'sector','axial'}, use_global_device_ids=true, to_apply=%region_7.8 | all-reduce | flops 256 | bytes 2048 | tf_op jit(solution)/shard_map/psum | solution.py:86
  336.9 38.0 %psum.44 = f32[128]{0:T(128)S(1)} all-reduce(f32[128]{0:T(128)S(1)} %get-tuple-element.6), channel_id=1, replica_groups=mesh['sector'=4,'axial'=8] {'sector','axial'}, use_global_device_ids=true, to_apply=%region_11.12 | all-reduce | flops 128 | bytes 1024 | tf_op jit(solution)/shard_map/psum | solution.py:86
  395.7 4.8 collective-permute-done.8
  406.4 9.3 %collective-permute-done.9 = f32[16,64,128]{2,1,0:T(8,128)S(1)} collective-permute-done((f32[16,64,128]{2,1,0:T(8,128)S(1)}, f32[16,64,128]{2,1,0:T(8,128)S(1)}, u32[]{:S(2)}, u32[]{:S(2)}) %collective-permute-start.9) | collective-permute-done | bytes 524320 | tf_op jit(solution)/shard_map/ppermute | solution.py:12
  416.9 13.9 %multiply_reduce_fusion.2 = (f32[128]{0:T(128)S(1)}, f32[64,64,128]{2,1,0:T(8,128)}) fusion(f32[64,64,128]{2,1,0:T(8,128)S(1)} %copy-done.1, f32[64,64,128]{2,0,1:T(8,128)S(1)} %fusion.28, f32[64,64,128]{2,0,1:T(8,128)S(1)} %fusion.30, f32[64,64,128]{2,0,1:T(8,128)S(1)} %fusion.32, f32[64,64,128]{2,0,1:T(8,128)S(1)} %fusion.34, ...), kind=kOutput, calls=%fused_computation.44 | convolution fusion | flops 406847360 | bytes 13648384 | tf_op jit(solution)/shard_map/pij,pjr->pir/dot_general | solution.py:95
  430.8 44.4 %psum.45 = f32[128]{0:T(128)S(1)} all-reduce(f32[128]{0:T(128)S(1)} %get-tuple-element.20), channel_id=1, replica_groups=mesh['sector'=4,'axial'=8] {'sector','axial'}, use_global_device_ids=true, to_apply=%region_13.14 | all-reduce | flops 128 | bytes 1024 | tf_op jit(solution)/shard_map/psum | solution.py:114
  478.6 38.0 %psum.46 = f32[128]{0:T(128)S(1)} all-reduce(f32[128]{0:T(128)S(1)} %get-tuple-element.4), channel_id=1, replica_groups=mesh['sector'=4,'axial'=8] {'sector','axial'}, use_global_device_ids=true, to_apply=%region_15.16 | all-reduce | flops 128 | bytes 1024 | tf_op jit(solution)/shard_map/psum | solution.py:86
  516.6 3.6 multiply_add_fusion.1
  537.9 4.8 collective-permute-done.12
  548.6 9.3 %collective-permute-done.13 = f32[16,64,128]{2,1,0:T(8,128)S(1)} collective-permute-done((f32[16,64,128]{2,1,0:T(8,128)S(1)}, f32[16,64,128]{2,1,0:T(8,128)S(1)}, u32[]{:S(2)}, u32[]{:S(2)}) %collective-permute-start.13) | collective-permute-done | bytes 524320 | tf_op jit(solution)/shard_map/ppermute | solution.py:12
  559.0 13.9 %multiply_reduce_fusion = (f32[128]{0:T(128)S(1)}, f32[64,64,128]{2,1,0:T(8,128)}) fusion(f32[64,64,128]{2,1,0:T(8,128)S(1)} %copy-done.5, f32[64,64,128]{2,0,1:T(8,128)S(1)} %fusion.20, f32[64,64,128]{2,0,1:T(8,128)S(1)} %fusion.22, f32[64,64,128]{2,0,1:T(8,128)S(1)} %fusion.24, f32[64,64,128]{2,0,1:T(8,128)S(1)} %fusion.26, ...), kind=kOutput, calls=%fused_computation.40 | convolution fusion | flops 406847360 | bytes 13648384 | tf_op jit(solution)/shard_map/pij,pjr->pir/dot_general | solution.py:95
  572.9 44.1 %psum.47 = f32[128]{0:T(128)S(1)} all-reduce(f32[128]{0:T(128)S(1)} %get-tuple-element.22), channel_id=1, replica_groups=mesh['sector'=4,'axial'=8] {'sector','axial'}, use_global_device_ids=true, to_apply=%region_17.18 | all-reduce | flops 128 | bytes 1024 | tf_op jit(solution)/shard_map/psum | solution.py:114
  617.1 5.3 multiply_subtract_fusion
  (130 shorter events, 115.4 us)
Async XLA Ops:
  5.4 11.0 %all-to-all-start.1 = ((s32[32,8,1]{1,2,0:T(1,128)}), s32[32,8,1]{1,2,0:T(1,128)S(1)}, u32[]{:S(2)}, u32[]{:S(2)}) async-start(s32[32,8,1]{1,2,0:T(1,128)} %bitcast.5), calls=%async_computation.1 | async-start | bytes 32768 | tf_op jit(solution)/shard_map/all_to_all | solution.py:55
  16.4 12.0 %all-to-all-start = ((s32[32,8,1]{1,2,0:T(1,128)}), s32[32,8,1]{1,2,0:T(1,128)S(1)}, u32[]{:S(2)}, u32[]{:S(2)}) async-start(s32[32,8,1]{1,2,0:T(1,128)} %bitcast.3), calls=%async_computation | async-start | bytes 32768 | tf_op jit(solution)/shard_map/all_to_all | solution.py:54
  21.0 5.6 copy-start.8
  28.3 47.2 %all-to-all-start.2 = ((s32[32,1,512]{2,1,0:T(1,128)}), s32[32,1,512]{2,1,0:T(1,128)S(1)}, u32[]{:S(2)}, u32[]{:S(2)}) async-start(s32[32,1,512]{2,1,0:T(1,128)} %reshape.290), calls=%async_computation.2 | async-start | bytes 131072 | tf_op jit(solution)/shard_map/all_to_all | solution.py:53
  75.5 5.9 copy-start.7
  75.5 7.5 %copy-start.10 = (s32[2,16,2]{1,2,0:T(2,128)S(1)}, s32[2,16,2]{1,2,0:T(2,128)}, u32[]{:S(2)}) copy-start(s32[2,16,2]{1,2,0:T(2,128)} %param.17) | copy-start | bytes 772
  75.5 14.8 %copy-start.9 = (f32[4096]{0:T(1024)S(1)}, f32[4096]{0:T(1024)}, u32[]{:S(2)}) copy-start(f32[4096]{0:T(1024)} %param.16) | copy-start | bytes 49156
  75.6 96.7 %all-to-all-start.3 = ((f32[32,1,32768]{2,1,0:T(1,128)}), f32[32,1,32768]{2,1,0:T(1,128)}, u32[]{:S(2)}, u32[]{:S(2)}) async-start(f32[32,1,32768]{2,1,0:T(1,128)} %reshape.288), calls=%async_computation.3 | async-start | bytes 8388608 | tf_op jit(solution)/shard_map/all_to_all | solution.py:52
  81.5 148.4 %collective-permute-start.1 = (f32[16,64]{1,0:T(8,128)S(1)}, f32[16,64]{1,0:T(8,128)S(1)}, u32[]{:S(2)}, u32[]{:S(2)}) collective-permute-start(f32[16,64]{1,0:T(8,128)S(1)} %get-tuple-element.9), channel_id=1, source_target_pairs={{0,8},{8,16},{16,24},{24,0},{1,9},{9,17},{17,25},{25,1},{2,10},{10... | collective-permute-start | bytes 12296 | tf_op jit(solution)/shard_map/ppermute | solution.py:12
  83.0 146.8 %collective-permute-start = (s32[16]{0:T(128)S(1)}, s32[16]{0:T(128)S(1)}, u32[]{:S(2)}, u32[]{:S(2)}) collective-permute-start(s32[16]{0:T(128)S(1)} %get-tuple-element.13), channel_id=1, source_target_pairs={{0,8},{8,16},{16,24},{24,0},{1,9},{9,17},{17,25},{25,1},{2,10},{10... | collective-permute-start | bytes 200 | tf_op jit(solution)/shard_map/ppermute | solution.py:12
  84.6 145.6 %collective-permute-start.3 = (f32[16,64]{1,0:T(8,128)S(1)}, f32[16,64]{1,0:T(8,128)S(1)}, u32[]{:S(2)}, u32[]{:S(2)}) collective-permute-start(f32[16,64]{1,0:T(8,128)S(1)} %get-tuple-element.8), channel_id=1, source_target_pairs={{0,1},{1,2},{2,3},{3,4},{4,5},{5,6},{6,7},{8,9},{9,10},{10,11},{11... | collective-permute-start | bytes 12296 | tf_op jit(solution)/shard_map/ppermute | solution.py:18
  86.5 17.3 %collective-permute-start.2 = (s32[16]{0:T(128)S(1)}, s32[16]{0:T(128)S(1)}, u32[]{:S(2)}, u32[]{:S(2)}) collective-permute-start(s32[16]{0:T(128)S(1)} %get-tuple-element.12), channel_id=1, source_target_pairs={{0,1},{1,2},{2,3},{3,4},{4,5},{5,6},{6,7},{8,9},{9,10},{10,11},{11... | collective-permute-start | bytes 200 | tf_op jit(solution)/shard_map/ppermute | solution.py:18
  224.9 5.6 copy-start
  235.1 13.5 %collective-permute-start.6 = (f32[16,64,128]{2,1,0:T(8,128)}, f32[16,64,128]{2,1,0:T(8,128)}, u32[]{:S(2)}, u32[]{:S(2)}) collective-permute-start(f32[16,64,128]{2,1,0:T(8,128)} %gather_fusion.4), channel_id=1, source_target_pairs={{1,0},{2,1},{3,2},{4,3},{5,4},{6,5},{7,6},{9,8},{10,9},{11,10},{12... | collective-permute-start | bytes 1572872 | tf_op jit(solution)/shard_map/ppermute | solution.py:18
  245.4 14.7 %collective-permute-start.4 = (f32[16,64,128]{2,1,0:T(8,128)}, f32[16,64,128]{2,1,0:T(8,128)S(1)}, u32[]{:S(2)}, u32[]{:S(2)}) collective-permute-start(f32[16,64,128]{2,1,0:T(8,128)} %gather_fusion.2), channel_id=1, source_target_pairs={{0,24},{8,0},{16,8},{24,16},{1,25},{9,1},{17,9},{25,17},{2,26},{10... | collective-permute-start | bytes 1572872 | tf_op jit(solution)/shard_map/ppermute | solution.py:12
  249.9 14.5 %collective-permute-start.7 = (f32[16,64,128]{2,1,0:T(8,128)S(1)}, f32[16,64,128]{2,1,0:T(8,128)S(1)}, u32[]{:S(2)}, u32[]{:S(2)}) collective-permute-start(f32[16,64,128]{2,1,0:T(8,128)S(1)} %subtract_multiply_fusion.4), channel_id=1, source_target_pairs={{0,1},{1,2},{2,3},{3,4},{4,5},{5,6},{6,7},{8,9},{9,10},{10,11},{11... | collective-permute-start | bytes 1572872 | tf_op jit(solution)/shard_map/ppermute | solution.py:18
  260.4 14.7 %collective-permute-start.5 = (f32[16,64,128]{2,1,0:T(8,128)S(1)}, f32[16,64,128]{2,1,0:T(8,128)S(1)}, u32[]{:S(2)}, u32[]{:S(2)}) collective-permute-start(f32[16,64,128]{2,1,0:T(8,128)S(1)} %subtract_multiply_fusion.5), channel_id=1, source_target_pairs={{0,8},{8,16},{16,24},{24,0},{1,9},{9,17},{17,25},{25,1},{2,10},{10... | collective-permute-start | bytes 1572872 | tf_op jit(solution)/shard_map/ppermute | solution.py:12
  264.4 11.9 %copy-start.2 = (f32[64,64,64]{2,0,1:T(8,128)S(1)}, f32[64,64,64]{2,0,1:T(8,128)}, u32[]{:S(2)}) copy-start(f32[64,64,64]{2,0,1:T(8,128)} %fusion) | copy-start | bytes 3145732
  264.4 11.9 %copy-start.6 = (f32[64,64,128]{2,1,0:T(8,128)S(1)}, f32[64,64,128]{2,1,0:T(8,128)}, u32[]{:S(2)}) copy-start(f32[64,64,128]{2,1,0:T(8,128)} %broadcast_divide_fusion) | copy-start | bytes 6291460
  381.0 11.3 %collective-permute-start.10 = (f32[16,64,128]{2,1,0:T(8,128)}, f32[16,64,128]{2,1,0:T(8,128)}, u32[]{:S(2)}, u32[]{:S(2)}) collective-permute-start(f32[16,64,128]{2,1,0:T(8,128)} %gather_fusion.8), channel_id=1, source_target_pairs={{1,0},{2,1},{3,2},{4,3},{5,4},{6,5},{7,6},{9,8},{10,9},{11,10},{12... | collective-permute-start | bytes 1572872 | tf_op jit(solution)/shard_map/ppermute | solution.py:18
  385.8 14.6 %collective-permute-start.8 = (f32[16,64,128]{2,1,0:T(8,128)}, f32[16,64,128]{2,1,0:T(8,128)}, u32[]{:S(2)}, u32[]{:S(2)}) collective-permute-start(f32[16,64,128]{2,1,0:T(8,128)} %gather_fusion.6), channel_id=1, source_target_pairs={{0,24},{8,0},{16,8},{24,16},{1,25},{9,1},{17,9},{25,17},{2,26},{10... | collective-permute-start | bytes 1572872 | tf_op jit(solution)/shard_map/ppermute | solution.py:12
  393.5 11.7 %collective-permute-start.11 = (f32[16,64,128]{2,1,0:T(8,128)S(1)}, f32[16,64,128]{2,1,0:T(8,128)S(1)}, u32[]{:S(2)}, u32[]{:S(2)}) collective-permute-start(f32[16,64,128]{2,1,0:T(8,128)S(1)} %subtract_multiply_fusion.2), channel_id=1, source_target_pairs={{0,1},{1,2},{2,3},{3,4},{4,5},{5,6},{6,7},{8,9},{9,10},{10,11},{11... | collective-permute-start | bytes 1572872 | tf_op jit(solution)/shard_map/ppermute | solution.py:18
  401.7 14.0 %collective-permute-start.9 = (f32[16,64,128]{2,1,0:T(8,128)S(1)}, f32[16,64,128]{2,1,0:T(8,128)S(1)}, u32[]{:S(2)}, u32[]{:S(2)}) collective-permute-start(f32[16,64,128]{2,1,0:T(8,128)S(1)} %subtract_multiply_fusion.3), channel_id=1, source_target_pairs={{0,8},{8,16},{16,24},{24,0},{1,9},{9,17},{17,25},{25,1},{2,10},{10... | collective-permute-start | bytes 1572872 | tf_op jit(solution)/shard_map/ppermute | solution.py:12
  405.2 11.7 %copy-start.1 = (f32[64,64,128]{2,1,0:T(8,128)S(1)}, f32[64,64,128]{2,1,0:T(8,128)}, u32[]{:S(2)}) copy-start(f32[64,64,128]{2,1,0:T(8,128)} %multiply_add_fusion.2) | copy-start | bytes 6291460
  405.2 11.7 %copy-start.3 = (f32[64,64,64]{2,0,1:T(8,128)S(1)}, f32[64,64,64]{2,0,1:T(8,128)}, u32[]{:S(2)}) copy-start(f32[64,64,64]{2,0,1:T(8,128)} %fusion) | copy-start | bytes 3145732
  523.1 11.4 %collective-permute-start.14 = (f32[16,64,128]{2,1,0:T(8,128)}, f32[16,64,128]{2,1,0:T(8,128)}, u32[]{:S(2)}, u32[]{:S(2)}) collective-permute-start(f32[16,64,128]{2,1,0:T(8,128)} %gather_fusion.12), channel_id=1, source_target_pairs={{1,0},{2,1},{3,2},{4,3},{5,4},{6,5},{7,6},{9,8},{10,9},{11,10},{12... | collective-permute-start | bytes 1572872 | tf_op jit(solution)/shard_map/ppermute | solution.py:18
  528.0 14.6 %collective-permute-start.12 = (f32[16,64,128]{2,1,0:T(8,128)}, f32[16,64,128]{2,1,0:T(8,128)}, u32[]{:S(2)}, u32[]{:S(2)}) collective-permute-start(f32[16,64,128]{2,1,0:T(8,128)} %gather_fusion.10), channel_id=1, source_target_pairs={{0,24},{8,0},{16,8},{24,16},{1,25},{9,1},{17,9},{25,17},{2,26},{10... | collective-permute-start | bytes 1572872 | tf_op jit(solution)/shard_map/ppermute | solution.py:12
  535.7 11.7 %collective-permute-start.15 = (f32[16,64,128]{2,1,0:T(8,128)S(1)}, f32[16,64,128]{2,1,0:T(8,128)S(1)}, u32[]{:S(2)}, u32[]{:S(2)}) collective-permute-start(f32[16,64,128]{2,1,0:T(8,128)S(1)} %subtract_multiply_fusion), channel_id=1, source_target_pairs={{0,1},{1,2},{2,3},{3,4},{4,5},{5,6},{6,7},{8,9},{9,10},{10,11},{11... | collective-permute-start | bytes 1572872 | tf_op jit(solution)/shard_map/ppermute | solution.py:18
  543.9 14.0 %collective-permute-start.13 = (f32[16,64,128]{2,1,0:T(8,128)S(1)}, f32[16,64,128]{2,1,0:T(8,128)S(1)}, u32[]{:S(2)}, u32[]{:S(2)}) collective-permute-start(f32[16,64,128]{2,1,0:T(8,128)S(1)} %subtract_multiply_fusion.1), channel_id=1, source_target_pairs={{0,8},{8,16},{16,24},{24,0},{1,9},{9,17},{17,25},{25,1},{2,10},{10... | collective-permute-start | bytes 1572872 | tf_op jit(solution)/shard_map/ppermute | solution.py:12
  547.4 11.6 %copy-start.4 = (f32[64,64,64]{2,0,1:T(8,128)S(1)}, f32[64,64,64]{2,0,1:T(8,128)}, u32[]{:S(2)}) copy-start(f32[64,64,64]{2,0,1:T(8,128)} %fusion) | copy-start | bytes 3145732
  547.4 11.6 %copy-start.5 = (f32[64,64,128]{2,1,0:T(8,128)S(1)}, f32[64,64,128]{2,1,0:T(8,128)}, u32[]{:S(2)}) copy-start(f32[64,64,128]{2,1,0:T(8,128)} %multiply_add_fusion.1) | copy-start | bytes 6291460
where the time goes:
time: 633 us; the launch traced here: 623 us
  blocking collectives  208 us (33%)
  waiting for transfers between devices  128 us (20%)
  matrix products  95.7 us (15%)
  local copies, waits for them, and re-layouts  89.1 us (14%)
  starting transfers between devices  54.6 us (9%)
  other arithmetic  44.9 us (7%)
    psum x3, blocking collectives, precond_sum(): lax.psum(jnp.sum(remaining_imbalance * precond, axis=(0, 1)), ('sector',...  120 us
    psum x2, blocking collectives, shards(): lax.psum(jnp.sum(update_vector * result, axis=(0, 1)), ('sector', 'axial'))  88.5 us
    all_to_all x1, waiting for transfers between devices, shards(): lax.all_to_all(send_blocks, ('sector', 'axial'), split_axis=0, concat_axi...  65.6 us
    ppermute x8, waiting for transfers between devices, from_behind(): lax.ppermute(array, axis, [(i, (i + by) % length) for i in range(length)])  45.7 us
    dot_general x3, matrix products, shards(): jnp.einsum('pij,pjr->pir', assembled, update_vector, precision=highest)  41.7 us
    unnamed x28, local copies, waits for them, and re-layouts  23.7 us
    scatter x1, local copies, waits for them, and re-layouts, shards(): jnp.zeros((total_slots, bound_nodes, bound_nodes), jnp.float32).at[target]  19.3 us
    ppermute x8, starting transfers between devices, shifted(): return lax.ppermute(block, axis, route)  18.4 us
  transfers between devices with their start and end apart: 20, of which 9 were waited for; matrix products, arithmetic and copies ran while one was open for 24% of the time, Pallas kernels for 0%

commit v1 on v0

--- a/solution.py
+++ b/solution.py
@@ -112,7 +112,7 @@
             - spread_field(axial_in_far, passed, patch_dev)
         )
         update_factor = norm_now / lax.psum(
-            jnp.sum(update_vector * result, axis=(0, 1)), ("sector", "axial")
+            lax.psum(jnp.sum(update_vector * result, axis=(0, 1)), "axial"), "sector"
         )
         current_estimate = current_estimate + update_factor * update_vector
         remaining_imbalance = remaining_imbalance - update_factor * result

time: 633 us -> 612 us (0.967)
  the two profiles are of different devices: /device:TPU:10 before, /device:TPU:0 now
where the time goes in v1:
time: 612 us; the launch traced here: 602 us
  blocking collectives  189 us (31%)
  waiting for transfers between devices  128 us (21%)
  matrix products  95.9 us (16%)
  local copies, waits for them, and re-layouts  89.2 us (15%)
  starting transfers between devices  51.2 us (8%)
  other arithmetic  45.9 us (8%)
    psum x3, blocking collectives, precond_sum(): lax.psum(jnp.sum(remaining_imbalance * precond, axis=(0, 1)), ('sector',...  119 us
    all_to_all x1, waiting for transfers between devices, shards(): lax.all_to_all(send_blocks, ('sector', 'axial'), split_axis=0, concat_axi...  81.8 us
    psum x3, blocking collectives, shards(): lax.psum(jnp.sum(update_vector * result, axis=(0, 1)), 'axial')  43.2 us
    dot_general x3, matrix products, shards(): jnp.einsum('pij,pjr->pir', assembled, update_vector, precision=highest)  41.7 us
    ppermute x8, waiting for transfers between devices, from_behind(): lax.ppermute(array, axis, [(i, (i + by) % length) for i in range(length)])  41.1 us
    psum x3, blocking collectives, shards(): lax.psum(lax.psum(jnp.sum(update_vector * result, axis=(0, 1)), 'axial'),...  27.3 us
    unnamed x28, local copies, waits for them, and re-layouts  23.7 us
    scatter x1, local copies, waits for them, and re-layouts, shards(): jnp.zeros((total_slots, bound_nodes, bound_nodes), jnp.float32).at[target]  19.4 us
  transfers between devices with their start and end apart: 20, of which 8 were waited for; matrix products, arithmetic and copies ran while one was open for 25% of the time, Pallas kernels for 0%

profile of v1, /device:TPU:0, one launch (start us, length us, event | category | flops | bytes accessed | tf_op | source)
XLA Modules:
  0.0 602.0 jit_solution(2789653582618781558)
XLA Ops:
  5.4 7.3 %all-to-all-start.1 = ((s32[32,8,1]{1,2,0:T(1,128)}), s32[32,8,1]{1,2,0:T(1,128)S(1)}, u32[]{:S(2)}, u32[]{:S(2)}) async-start(s32[32,8,1]{1,2,0:T(1,128)} %bitcast.5), calls=%async_computation.1 | async-start | bytes 32768 | tf_op jit(solution)/shard_map/all_to_all | solution.py:55
  14.5 5.3 all-to-all-done.1
  22.3 5.6 copy.75
  29.7 5.8 all-to-all-start.2
  35.5 7.9 %convolution_subtract_fusion = f32[128,64,64]{2,1,0:T(8,128)} fusion(f32[128,64,64]{2,1,0:T(8,128)} %copy.75, bf16[128,256,64]{1,2,0:T(8,128)(2,1)} %param.11), kind=kOutput, calls=%fused_computation.25 | convolution fusion | flops 268959744 | bytes 8388608 | tf_op jit(solution)/shard_map/eib,eic->ebc/dot_general | solution.py:40
  43.4 4.3 broadcast_in_dim.11
  47.7 19.4 %scatter_fusion = f32[256,64,64]{2,1,0:T(8,128)} fusion(f32[256,64,64]{2,1,0:T(8,128)} %broadcast_in_dim.11, s32[128]{0:T(128)S(1)} %fusion.85, f32[128,64,64]{2,1,0:T(8,128)} %convolution_subtract_fusion), kind=kCustom, calls=%fused_computation.16 | custom fusion | bytes 6291968 | tf_op jit(solution)/shard_map/scatter | solution.py:46
  67.1 9.8 %reshape.288 = f32[32,1,32768]{2,1,0:T(1,128)} reshape(f32[256,64,64]{2,1,0:T(8,128)} %scatter_fusion) | data formatting | bytes 8388608
  76.9 5.9 all-to-all-start.3
  95.1 81.8 %all-to-all-done.3 = f32[32,1,32768]{2,1,0:T(1,128)} async-done(((f32[32,1,32768]{2,1,0:T(1,128)}), f32[32,1,32768]{2,1,0:T(1,128)}, u32[]{:S(2)}, u32[]{:S(2)}) %all-to-all-start.3) | async-done | bytes 4194336 | tf_op jit(solution)/shard_map/all_to_all | solution.py:52
  177.4 13.7 %reduce.9 = f32[32,32768]{1,0:T(8,128)} reduce(f32[32,1,32768]{2,1,0:T(1,128)} %all-to-all-done.3, f32[]{:T(128)} %broadcast.166), dimensions={1}, to_apply=%all_to_all.27.reduce_sub_computation | reduce | bytes 8388612 | tf_op jit(solution)/shard_map/all_to_all | solution.py:52
  191.1 7.4 %reshape.289 = f32[256,64,64]{2,1,0:T(8,128)} reshape(f32[32,32768]{1,0:T(8,128)} %reduce.9) | data formatting | bytes 8388608
  198.5 11.8 %fusion.3 = f32[256,64,64]{2,1,0:T(8,128)S(1)} fusion(f32[256,64,64]{2,1,0:T(8,128)} %reshape.289, s32[256,64]{1,0:T(8,128)S(1)} %bitcast.83), kind=kOutput, calls=%fused_computation.21 | convolution fusion | flops 806354944 | bytes 8454144 | tf_op jit(solution)/shard_map/rsj,rst->rjt/dot_general | solution.py:60
  210.3 8.4 %fusion.2 = f32[256,64,64]{2,1,0:T(8,128)S(1)} fusion(f32[256,64,64]{2,1,0:T(8,128)S(1)} %fusion.3, s32[256,64]{1,0:T(8,128)S(1)} %bitcast.84), kind=kOutput, calls=%fused_computation.20 | convolution fusion | flops 806354944 | bytes 8454144 | tf_op jit(solution)/shard_map/rjt,rtk->rjk/dot_general | solution.py:61
  218.8 11.0 %fusion = f32[64,64,64]{2,0,1:T(8,128)} fusion(f32[256,64,64]{2,1,0:T(8,128)S(1)} %fusion.2, f32[256]{0:T(256)S(1)} %convert_element_type.50, s32[256]{0:T(256)S(1)} %eq.56), kind=kOutput, calls=%fused_computation.17 | convolution fusion | flops 805339136 | bytes 5244928 | tf_op jit(solution)/shard_map/rp,rjk->pjk/dot_general | solution.py:63
  251.4 39.4 %psum.63 = f32[128]{0:T(128)S(1)} all-reduce(f32[128]{0:T(128)S(1)} %fusion.6), channel_id=1, replica_groups=mesh['sector'=4,'axial'=8] {'sector','axial'}, use_global_device_ids=true, to_apply=%region_7.8 | all-reduce | flops 128 | bytes 1024 | tf_op jit(solution)/shard_map/psum | solution.py:86
  300.1 9.4 %collective-permute-done.5 = f32[16,64,128]{2,1,0:T(8,128)S(1)} collective-permute-done((f32[16,64,128]{2,1,0:T(8,128)S(1)}, f32[16,64,128]{2,1,0:T(8,128)S(1)}, u32[]{:S(2)}, u32[]{:S(2)}) %collective-permute-start.5) | collective-permute-done | bytes 524320 | tf_op jit(solution)/shard_map/ppermute | solution.py:12
  310.6 13.9 %multiply_reduce_fusion.4 = (f32[128]{0:T(128)S(1)}, f32[64,64,128]{2,1,0:T(8,128)}) fusion(f32[64,64,128]{2,1,0:T(8,128)S(1)} %copy-done.6, f32[64,64,128]{2,0,1:T(8,128)S(1)} %fusion.36, f32[64,64,128]{2,0,1:T(8,128)S(1)} %fusion.38, f32[64,64,128]{2,0,1:T(8,128)S(1)} %fusion.40, f32[64,64,128]{2,0,1:T(8,128)S(1)} %fusion.42, ...), kind=kOutput, calls=%fused_computation.48 | convolution fusion | flops 406847360 | bytes 13648384 | tf_op jit(solution)/shard_map/pij,pjr->pir/dot_general | solution.py:95
  324.5 14.6 %psum.64 = f32[128]{0:T(128)S(1)} all-reduce(f32[128]{0:T(128)S(1)} %get-tuple-element.16), channel_id=1, replica_groups=mesh['sector'=4,'axial'=8] {'axial'}, use_global_device_ids=true, to_apply=%region_9.10 | all-reduce | flops 128 | bytes 1024 | tf_op jit(solution)/shard_map/psum | solution.py:115
  339.1 8.4 %psum.65 = f32[128]{0:T(128)S(1)} all-reduce(f32[128]{0:T(128)S(1)} %psum.64), channel_id=1, replica_groups=mesh['sector'=4,'axial'=8] {'sector'}, use_global_device_ids=true, to_apply=%region_10.11 | all-reduce | flops 128 | bytes 1024 | tf_op jit(solution)/shard_map/psum | solution.py:114
  350.3 40.7 %psum.66 = f32[128]{0:T(128)S(1)} all-reduce(f32[128]{0:T(128)S(1)} %get-tuple-element.4), channel_id=1, replica_groups=mesh['sector'=4,'axial'=8] {'sector','axial'}, use_global_device_ids=true, to_apply=%region_12.13 | all-reduce | flops 128 | bytes 1024 | tf_op jit(solution)/shard_map/psum | solution.py:86
  421.5 12.2 %collective-permute-done.9 = f32[16,64,128]{2,1,0:T(8,128)S(1)} collective-permute-done((f32[16,64,128]{2,1,0:T(8,128)S(1)}, f32[16,64,128]{2,1,0:T(8,128)S(1)}, u32[]{:S(2)}, u32[]{:S(2)}) %collective-permute-start.9) | collective-permute-done | bytes 524320 | tf_op jit(solution)/shard_map/ppermute | solution.py:12
  434.9 13.9 %multiply_reduce_fusion.2 = (f32[128]{0:T(128)S(1)}, f32[64,64,128]{2,1,0:T(8,128)}) fusion(f32[64,64,128]{2,1,0:T(8,128)S(1)} %copy-done.1, f32[64,64,128]{2,0,1:T(8,128)S(1)} %fusion.28, f32[64,64,128]{2,0,1:T(8,128)S(1)} %fusion.30, f32[64,64,128]{2,0,1:T(8,128)S(1)} %fusion.32, f32[64,64,128]{2,0,1:T(8,128)S(1)} %fusion.34, ...), kind=kOutput, calls=%fused_computation.44 | convolution fusion | flops 406847360 | bytes 13648384 | tf_op jit(solution)/shard_map/pij,pjr->pir/dot_general | solution.py:95
  448.8 15.3 %psum.67 = f32[128]{0:T(128)S(1)} all-reduce(f32[128]{0:T(128)S(1)} %get-tuple-element.18), channel_id=1, replica_groups=mesh['sector'=4,'axial'=8] {'axial'}, use_global_device_ids=true, to_apply=%region_14.15 | all-reduce | flops 128 | bytes 1024 | tf_op jit(solution)/shard_map/psum | solution.py:115
  464.1 9.5 %psum.68 = f32[128]{0:T(128)S(1)} all-reduce(f32[128]{0:T(128)S(1)} %psum.67), channel_id=1, replica_groups=mesh['sector'=4,'axial'=8] {'sector'}, use_global_device_ids=true, to_apply=%region_15.16 | all-reduce | flops 128 | bytes 1024 | tf_op jit(solution)/shard_map/psum | solution.py:114
  477.1 38.5 %psum.69 = f32[128]{0:T(128)S(1)} all-reduce(f32[128]{0:T(128)S(1)} %get-tuple-element.2), channel_id=1, replica_groups=mesh['sector'=4,'axial'=8] {'sector','axial'}, use_global_device_ids=true, to_apply=%region_17.18 | all-reduce | flops 128 | bytes 1024 | tf_op jit(solution)/shard_map/psum | solution.py:86
  537.0 4.3 collective-permute-done.12
  547.6 11.0 %collective-permute-done.13 = f32[16,64,128]{2,1,0:T(8,128)S(1)} collective-permute-done((f32[16,64,128]{2,1,0:T(8,128)S(1)}, f32[16,64,128]{2,1,0:T(8,128)S(1)}, u32[]{:S(2)}, u32[]{:S(2)}) %collective-permute-start.13) | collective-permute-done | bytes 524320 | tf_op jit(solution)/shard_map/ppermute | solution.py:12
  559.7 13.9 %multiply_reduce_fusion = (f32[128]{0:T(128)S(1)}, f32[64,64,128]{2,1,0:T(8,128)}) fusion(f32[64,64,128]{2,1,0:T(8,128)S(1)} %copy-done.5, f32[64,64,128]{2,0,1:T(8,128)S(1)} %fusion.20, f32[64,64,128]{2,0,1:T(8,128)S(1)} %fusion.22, f32[64,64,128]{2,0,1:T(8,128)S(1)} %fusion.24, f32[64,64,128]{2,0,1:T(8,128)S(1)} %fusion.26, ...), kind=kOutput, calls=%fused_computation.40 | convolution fusion | flops 406847360 | bytes 13648384 | tf_op jit(solution)/shard_map/pij,pjr->pir/dot_general | solution.py:95
  573.6 13.4 %psum.70 = f32[128]{0:T(128)S(1)} all-reduce(f32[128]{0:T(128)S(1)} %get-tuple-element.20), channel_id=1, replica_groups=mesh['sector'=4,'axial'=8] {'axial'}, use_global_device_ids=true, to_apply=%region_19.20 | all-reduce | flops 128 | bytes 1024 | tf_op jit(solution)/shard_map/psum | solution.py:115
  587.0 9.5 %psum.71 = f32[128]{0:T(128)S(1)} all-reduce(f32[128]{0:T(128)S(1)} %psum.70), channel_id=1, replica_groups=mesh['sector'=4,'axial'=8] {'sector'}, use_global_device_ids=true, to_apply=%region_20.21 | all-reduce | flops 128 | bytes 1024 | tf_op jit(solution)/shard_map/psum | solution.py:114
  596.5 5.3 multiply_subtract_fusion
  (134 shorter events, 121.5 us)
Async XLA Ops:
  5.4 14.4 %all-to-all-start.1 = ((s32[32,8,1]{1,2,0:T(1,128)}), s32[32,8,1]{1,2,0:T(1,128)S(1)}, u32[]{:S(2)}, u32[]{:S(2)}) async-start(s32[32,8,1]{1,2,0:T(1,128)} %bitcast.5), calls=%async_computation.1 | async-start | bytes 32768 | tf_op jit(solution)/shard_map/all_to_all | solution.py:55
  19.8 9.9 %all-to-all-start = ((s32[32,8,1]{1,2,0:T(1,128)}), s32[32,8,1]{1,2,0:T(1,128)S(1)}, u32[]{:S(2)}, u32[]{:S(2)}) async-start(s32[32,8,1]{1,2,0:T(1,128)} %bitcast.3), calls=%async_computation | async-start | bytes 32768 | tf_op jit(solution)/shard_map/all_to_all | solution.py:54
  22.3 5.6 copy-start.8
  29.7 47.2 %all-to-all-start.2 = ((s32[32,1,512]{2,1,0:T(1,128)}), s32[32,1,512]{2,1,0:T(1,128)S(1)}, u32[]{:S(2)}, u32[]{:S(2)}) async-start(s32[32,1,512]{2,1,0:T(1,128)} %reshape.290), calls=%async_computation.2 | async-start | bytes 131072 | tf_op jit(solution)/shard_map/all_to_all | solution.py:53
  76.9 5.9 copy-start.7
  76.9 7.7 %copy-start.10 = (s32[2,16,2]{1,2,0:T(2,128)S(1)}, s32[2,16,2]{1,2,0:T(2,128)}, u32[]{:S(2)}) copy-start(s32[2,16,2]{1,2,0:T(2,128)} %param.17) | copy-start | bytes 772
  76.9 14.9 %copy-start.9 = (f32[4096]{0:T(1024)S(1)}, f32[4096]{0:T(1024)}, u32[]{:S(2)}) copy-start(f32[4096]{0:T(1024)} %param.16) | copy-start | bytes 49156
  76.9 100.0 %all-to-all-start.3 = ((f32[32,1,32768]{2,1,0:T(1,128)}), f32[32,1,32768]{2,1,0:T(1,128)}, u32[]{:S(2)}, u32[]{:S(2)}) async-start(f32[32,1,32768]{2,1,0:T(1,128)} %reshape.288), calls=%async_computation.3 | async-start | bytes 8388608 | tf_op jit(solution)/shard_map/all_to_all | solution.py:52
  82.9 151.9 %collective-permute-start.1 = (f32[16,64]{1,0:T(8,128)S(1)}, f32[16,64]{1,0:T(8,128)S(1)}, u32[]{:S(2)}, u32[]{:S(2)}) collective-permute-start(f32[16,64]{1,0:T(8,128)S(1)} %get-tuple-element.7), channel_id=1, source_target_pairs={{0,8},{8,16},{16,24},{24,0},{1,9},{9,17},{17,25},{25,1},{2,10},{10... | collective-permute-start | bytes 12296 | tf_op jit(solution)/shard_map/ppermute | solution.py:12
  84.6 150.2 %collective-permute-start = (s32[16]{0:T(128)S(1)}, s32[16]{0:T(128)S(1)}, u32[]{:S(2)}, u32[]{:S(2)}) collective-permute-start(s32[16]{0:T(128)S(1)} %get-tuple-element.11), channel_id=1, source_target_pairs={{0,8},{8,16},{16,24},{24,0},{1,9},{9,17},{17,25},{25,1},{2,10},{10... | collective-permute-start | bytes 200 | tf_op jit(solution)/shard_map/ppermute | solution.py:12
  86.1 149.0 %collective-permute-start.3 = (f32[16,64]{1,0:T(8,128)S(1)}, f32[16,64]{1,0:T(8,128)S(1)}, u32[]{:S(2)}, u32[]{:S(2)}) collective-permute-start(f32[16,64]{1,0:T(8,128)S(1)} %get-tuple-element.6), channel_id=1, source_target_pairs={{0,1},{1,2},{2,3},{3,4},{4,5},{5,6},{6,7},{8,9},{9,10},{10,11},{11... | collective-permute-start | bytes 12296 | tf_op jit(solution)/shard_map/ppermute | solution.py:18
  87.6 4.7 collective-permute-start.2
  229.8 5.6 copy-start
  240.1 50.8 %collective-permute-start.6 = (f32[16,64,128]{2,1,0:T(8,128)}, f32[16,64,128]{2,1,0:T(8,128)}, u32[]{:S(2)}, u32[]{:S(2)}) collective-permute-start(f32[16,64,128]{2,1,0:T(8,128)} %gather_fusion.4), channel_id=1, source_target_pairs={{1,0},{2,1},{3,2},{4,3},{5,4},{6,5},{7,6},{9,8},{10,9},{11,10},{12... | collective-permute-start | bytes 1572872 | tf_op jit(solution)/shard_map/ppermute | solution.py:18
  248.8 44.8 %collective-permute-start.4 = (f32[16,64,128]{2,1,0:T(8,128)}, f32[16,64,128]{2,1,0:T(8,128)}, u32[]{:S(2)}, u32[]{:S(2)}) collective-permute-start(f32[16,64,128]{2,1,0:T(8,128)} %gather_fusion.2), channel_id=1, source_target_pairs={{0,24},{8,0},{16,8},{24,16},{1,25},{9,1},{17,9},{25,17},{2,26},{10... | collective-permute-start | bytes 1572872 | tf_op jit(solution)/shard_map/ppermute | solution.py:12
  292.1 6.8 %collective-permute-start.7 = (f32[16,64,128]{2,1,0:T(8,128)S(1)}, f32[16,64,128]{2,1,0:T(8,128)S(1)}, u32[]{:S(2)}, u32[]{:S(2)}) collective-permute-start(f32[16,64,128]{2,1,0:T(8,128)S(1)} %subtract_multiply_fusion.4), channel_id=1, source_target_pairs={{0,1},{1,2},{2,3},{3,4},{4,5},{5,6},{6,7},{8,9},{9,10},{10,11},{11... | collective-permute-start | bytes 1572872 | tf_op jit(solution)/shard_map/ppermute | solution.py:18
  294.9 14.6 %collective-permute-start.5 = (f32[16,64,128]{2,1,0:T(8,128)S(1)}, f32[16,64,128]{2,1,0:T(8,128)S(1)}, u32[]{:S(2)}, u32[]{:S(2)}) collective-permute-start(f32[16,64,128]{2,1,0:T(8,128)S(1)} %subtract_multiply_fusion.5), channel_id=1, source_target_pairs={{0,8},{8,16},{16,24},{24,0},{1,9},{9,17},{17,25},{25,1},{2,10},{10... | collective-permute-start | bytes 1572872 | tf_op jit(solution)/shard_map/ppermute | solution.py:12
  298.9 11.7 %copy-start.2 = (f32[64,64,64]{2,0,1:T(8,128)S(1)}, f32[64,64,64]{2,0,1:T(8,128)}, u32[]{:S(2)}) copy-start(f32[64,64,64]{2,0,1:T(8,128)} %fusion) | copy-start | bytes 3145732
  298.9 11.7 %copy-start.6 = (f32[64,64,128]{2,1,0:T(8,128)S(1)}, f32[64,64,128]{2,1,0:T(8,128)}, u32[]{:S(2)}) copy-start(f32[64,64,128]{2,1,0:T(8,128)} %broadcast_divide_fusion) | copy-start | bytes 6291460
  397.1 10.1 %collective-permute-start.10 = (f32[16,64,128]{2,1,0:T(8,128)}, f32[16,64,128]{2,1,0:T(8,128)}, u32[]{:S(2)}, u32[]{:S(2)}) collective-permute-start(f32[16,64,128]{2,1,0:T(8,128)} %gather_fusion.8), channel_id=1, source_target_pairs={{1,0},{2,1},{3,2},{4,3},{5,4},{6,5},{7,6},{9,8},{10,9},{11,10},{12... | collective-permute-start | bytes 1572872 | tf_op jit(solution)/shard_map/ppermute | solution.py:18
  401.3 15.0 %collective-permute-start.8 = (f32[16,64,128]{2,1,0:T(8,128)}, f32[16,64,128]{2,1,0:T(8,128)}, u32[]{:S(2)}, u32[]{:S(2)}) collective-permute-start(f32[16,64,128]{2,1,0:T(8,128)} %gather_fusion.6), channel_id=1, source_target_pairs={{0,24},{8,0},{16,8},{24,16},{1,25},{9,1},{17,9},{25,17},{2,26},{10... | collective-permute-start | bytes 1572872 | tf_op jit(solution)/shard_map/ppermute | solution.py:12
  408.4 11.9 %collective-permute-start.11 = (f32[16,64,128]{2,1,0:T(8,128)S(1)}, f32[16,64,128]{2,1,0:T(8,128)S(1)}, u32[]{:S(2)}, u32[]{:S(2)}) collective-permute-start(f32[16,64,128]{2,1,0:T(8,128)S(1)} %subtract_multiply_fusion.2), channel_id=1, source_target_pairs={{0,1},{1,2},{2,3},{3,4},{4,5},{5,6},{6,7},{8,9},{9,10},{10,11},{11... | collective-permute-start | bytes 1572872 | tf_op jit(solution)/shard_map/ppermute | solution.py:18
  417.5 16.2 %collective-permute-start.9 = (f32[16,64,128]{2,1,0:T(8,128)S(1)}, f32[16,64,128]{2,1,0:T(8,128)S(1)}, u32[]{:S(2)}, u32[]{:S(2)}) collective-permute-start(f32[16,64,128]{2,1,0:T(8,128)S(1)} %subtract_multiply_fusion.3), channel_id=1, source_target_pairs={{0,8},{8,16},{16,24},{24,0},{1,9},{9,17},{17,25},{25,1},{2,10},{10... | collective-permute-start | bytes 1572872 | tf_op jit(solution)/shard_map/ppermute | solution.py:12
  420.3 14.6 %copy-start.1 = (f32[64,64,128]{2,1,0:T(8,128)S(1)}, f32[64,64,128]{2,1,0:T(8,128)}, u32[]{:S(2)}) copy-start(f32[64,64,128]{2,1,0:T(8,128)} %multiply_add_fusion.2) | copy-start | bytes 6291460
  420.3 14.6 %copy-start.3 = (f32[64,64,64]{2,0,1:T(8,128)S(1)}, f32[64,64,64]{2,0,1:T(8,128)}, u32[]{:S(2)}) copy-start(f32[64,64,64]{2,0,1:T(8,128)} %fusion) | copy-start | bytes 3145732
  522.1 10.2 %collective-permute-start.14 = (f32[16,64,128]{2,1,0:T(8,128)}, f32[16,64,128]{2,1,0:T(8,128)}, u32[]{:S(2)}, u32[]{:S(2)}) collective-permute-start(f32[16,64,128]{2,1,0:T(8,128)} %gather_fusion.12), channel_id=1, source_target_pairs={{1,0},{2,1},{3,2},{4,3},{5,4},{6,5},{7,6},{9,8},{10,9},{11,10},{12... | collective-permute-start | bytes 1572872 | tf_op jit(solution)/shard_map/ppermute | solution.py:18
  526.4 15.0 %collective-permute-start.12 = (f32[16,64,128]{2,1,0:T(8,128)}, f32[16,64,128]{2,1,0:T(8,128)}, u32[]{:S(2)}, u32[]{:S(2)}) collective-permute-start(f32[16,64,128]{2,1,0:T(8,128)} %gather_fusion.10), channel_id=1, source_target_pairs={{0,24},{8,0},{16,8},{24,16},{1,25},{9,1},{17,9},{25,17},{2,26},{10... | collective-permute-start | bytes 1572872 | tf_op jit(solution)/shard_map/ppermute | solution.py:12
  533.5 12.8 %collective-permute-start.15 = (f32[16,64,128]{2,1,0:T(8,128)S(1)}, f32[16,64,128]{2,1,0:T(8,128)S(1)}, u32[]{:S(2)}, u32[]{:S(2)}) collective-permute-start(f32[16,64,128]{2,1,0:T(8,128)S(1)} %subtract_multiply_fusion), channel_id=1, source_target_pairs={{0,1},{1,2},{2,3},{3,4},{4,5},{5,6},{6,7},{8,9},{9,10},{10,11},{11... | collective-permute-start | bytes 1572872 | tf_op jit(solution)/shard_map/ppermute | solution.py:18
  542.6 16.0 %collective-permute-start.13 = (f32[16,64,128]{2,1,0:T(8,128)S(1)}, f32[16,64,128]{2,1,0:T(8,128)S(1)}, u32[]{:S(2)}, u32[]{:S(2)}) collective-permute-start(f32[16,64,128]{2,1,0:T(8,128)S(1)} %subtract_multiply_fusion.1), channel_id=1, source_target_pairs={{0,8},{8,16},{16,24},{24,0},{1,9},{9,17},{17,25},{25,1},{2,10},{10... | collective-permute-start | bytes 1572872 | tf_op jit(solution)/shard_map/ppermute | solution.py:12
  546.4 13.4 %copy-start.4 = (f32[64,64,64]{2,0,1:T(8,128)S(1)}, f32[64,64,64]{2,0,1:T(8,128)}, u32[]{:S(2)}) copy-start(f32[64,64,64]{2,0,1:T(8,128)} %fusion) | copy-start | bytes 3145732
  546.4 13.3 %copy-start.5 = (f32[64,64,128]{2,1,0:T(8,128)S(1)}, f32[64,64,128]{2,1,0:T(8,128)}, u32[]{:S(2)}) copy-start(f32[64,64,128]{2,1,0:T(8,128)} %multiply_add_fusion.1) | copy-start | bytes 6291460
